TPU v7x, 128 devices: a whole 4x4x4 slice. The times are simulated.
128 devices in a mesh: row: 16 (over z, y_hi, core), col: 8 (over y_lo, x).
Axes of the slice: x: 4, y: 4 (y_hi: 2, y_lo: 2; y = y_hi * 2 + y_lo), z: 4, core: 2. Of those that a mesh axis runs over, the one named last changes fastest.
Arguments:
- sky_image: bfloat16 [2, 16384, 16384], P(None, 'row', 'col'), may hold values from -6 to 6
- facet_rows: int32 [128], replicated, may hold values from 512 to 15872
- facet_offsets: int32 [128], replicated, may hold values from 0 to 127
- facet_owner: int32 [128], replicated, may hold values from 0 to 127, each once
Outputs:
- facets: bfloat16 [128, 2, 1024, 1024], P(('row', 'col'))
Inputs may be any that keep to these rules, and one draw needn't show every extreme that they name: `facet_owner`: the entries are distinct, so every device owns exactly one facet.
All inputs are finite; a program needn't handle non-finite values.
Results may differ from a plain program's by a relative error of at most 0.0095.
Values may be sent and summed in bfloat16 or wider, within the bound.
No kernel may reach another device: no remote copies, remote signals or barrier semaphores. Data moves between devices by JAX's collectives and lax.ppermute only.
A program may use at most 128 MiB of HBM per device.

v0:
```python
import math
import jax
import jax.numpy as jnp
from jax import lax
from jax.sharding import PartitionSpec as P

N = 16384
FS = 1024
SPLIT = 128


def split_up(shard, dim, devices):
    lengths = shard.shape
    parts = shard.reshape(*lengths[:dim], devices, lengths[dim] // devices, *lengths[dim + 1 :])
    return jnp.moveaxis(parts, dim, 0)


def edges_of(length, count):
    unit = 8 if length >= 8 * count else 1
    return [length // unit * k // count * unit for k in range(1, count)]


def joined_along(parts, dim):
    lengths = list(parts.shape[1:])
    lengths[dim] *= parts.shape[0]
    return jnp.moveaxis(parts, 0, dim).reshape(lengths)


def cut_exchange(shard, axis, pieces, split_dim, concat_dim):
    parts = split_up(shard, split_dim, lax.axis_size(axis))
    widest = max(range(1, max(2, parts.ndim - 1)), key=lambda d: parts.shape[d])
    gathered = []
    for share in jnp.split(parts, edges_of(parts.shape[widest], pieces), axis=widest):
        if share.size:
            gathered.append(lax.all_to_all(share, axis, split_axis=0, concat_axis=0, tiled=True))
    return joined_along(jnp.concatenate(gathered, axis=widest), concat_dim)


def shifted(block, axis, distance):
    devices = range(lax.axis_size(axis))
    route = [((i - distance) % len(devices), i) for i in devices]
    return lax.ppermute(block, axis, route)


def dft_table(length):
    positions = jnp.arange(length, dtype=jnp.int32)
    turn_count = positions[:, None] * positions[None, :] % length
    angles = turn_count.astype(jnp.float32) * (-2.0 * math.pi / length)
    factor = 1.0 / math.sqrt(length)
    return (
        (jnp.cos(angles) * factor).astype(jnp.bfloat16),
        (jnp.sin(angles) * factor).astype(jnp.bfloat16),
    )


def twiddle_table(first_len, second_len, total):
    left_index = jnp.arange(first_len, dtype=jnp.int32)[:, None]
    right_index = jnp.arange(second_len, dtype=jnp.int32)[None, :]
    angles = (left_index * right_index % total).astype(jnp.float32) * (-2.0 * math.pi / total)
    return (jnp.cos(angles), jnp.sin(angles))


def complex_mix(formula, tables, values):
    re_part = jnp.einsum(
        formula, tables[0], values[0], preferred_element_type=jnp.float32
    ) - jnp.einsum(formula, tables[1], values[1], preferred_element_type=jnp.float32)
    im_part = jnp.einsum(
        formula, tables[0], values[1], preferred_element_type=jnp.float32
    ) + jnp.einsum(formula, tables[1], values[0], preferred_element_type=jnp.float32)
    return (re_part, im_part)


def rotate(pair, twiddle):
    return (
        pair[0] * twiddle[0] - pair[1] * twiddle[1],
        pair[0] * twiddle[1] + pair[1] * twiddle[0],
    )


def as_stored(pair):
    return jnp.stack((pair[0].astype(jnp.bfloat16), pair[1].astype(jnp.bfloat16)))


def rows_pass(strip_rows):
    row_count = strip_rows.shape[1]
    lead_len = N // SPLIT
    blocks = strip_rows.reshape(2, row_count, lead_len, SPLIT)
    mixed_pair = complex_mix("pa,rab->rpb", dft_table(lead_len), (blocks[0], blocks[1]))
    section_one = as_stored(rotate(mixed_pair, twiddle_table(lead_len, SPLIT, N)))
    mixed_pair = complex_mix("qb,rpb->rqp", dft_table(SPLIT), (section_one[0], section_one[1]))
    return as_stored(mixed_pair).reshape(2, row_count, N)


def shards(sky_image, facet_rows, facet_offsets, facet_owner):
    strip_rows = lax.all_to_all(sky_image, "col", split_axis=1, concat_axis=2, tiled=True)
    rows_done = rows_pass(strip_rows)
    row_devices = lax.axis_size("row")
    col_devices = lax.axis_size("col")
    devices = row_devices * col_devices
    strip_len = rows_done.shape[1]
    tables = dft_table(devices)
    twiddle = twiddle_table(devices, strip_len, N)
    twiddle = (twiddle[0][:, :, None], twiddle[1][:, :, None])
    columns = cut_exchange(rows_done, ("row", "col"), 2, 2, 1)
    col_width = columns.shape[2]
    grouped = columns.reshape(2, devices, strip_len, col_width)
    mixed_pair = complex_mix("pg,gic->pic", tables, (grouped[0], grouped[1]))
    section_two = as_stored(rotate(mixed_pair, twiddle))
    mixed_pair = complex_mix("qi,pic->qpc", dft_table(strip_len), (section_two[0], section_two[1]))
    grid_cols = as_stored(mixed_pair).reshape(2, N, col_width)
    my_index = lax.axis_index(("row", "col"))
    device_ids = jnp.arange(devices, dtype=jnp.int32)
    matches = (facet_owner[None, :] == device_ids[:, None]).astype(jnp.int32)
    owned_count = jnp.sum(matches, axis=1)
    centre_row = jnp.where(owned_count > 0, jnp.sum(matches * facet_rows[None, :], axis=1), FS // 2)
    centre_col = jnp.sum(matches * facet_offsets[None, :], axis=1)
    reach_blocks = FS // (2 * col_width)
    pieces = []
    for distance in range(reach_blocks, -reach_blocks - 1, -1):
        target = (my_index + distance) % devices
        start_row = centre_row[target] - FS // 2
        band_rows = lax.dynamic_slice_in_dim(grid_cols, start_row, FS, 1)
        if distance != 0:
            band_rows = shifted(band_rows, ("row", "col"), distance)
        pieces.append(band_rows)
    window = jnp.concatenate(pieces, axis=2)
    facet_tile = lax.dynamic_slice_in_dim(window, centre_col[my_index], FS, 2)
    taper_axis = 0.25 + 0.75 * jnp.sin(math.pi * (jnp.arange(FS, dtype=jnp.float32) + 0.5) / FS)
    weight = taper_axis[:, None] * taper_axis[None, :] * owned_count[my_index].astype(jnp.float32)
    return (facet_tile.astype(jnp.float32) * weight).astype(jnp.bfloat16)[None]


def solution(mesh):
    placed = (P(None, "row", "col"), P(), P(), P())
    return jax.shard_map(
        shards,
        mesh=mesh,
        in_specs=placed,
        out_specs=P(("row", "col"), None, None, None),
        check_vma=False,
    )
```

profile of v0, /device:TPU:21, one launch (start us, length us, event | category | flops | bytes accessed | tf_op | source)
XLA Modules:
  0.0 524.7 jit_solution(18393274846443005914)
XLA Ops:
  0.0 16.4 %copy.29 = bf16[2,1024,2048]{2,0,1:T(2,128)(2,1)} copy(bf16[2,1024,2048]{2,1,0:T(8,128)(2,1)} %param.4) | data formatting | bytes 16777216 | tf_op args[0]
  21.8 114.8 %all-to-all-done = bf16[2,1024,2048]{2,0,1:T(2,128)(2,1)} async-done(((bf16[2,1024,2048]{2,0,1:T(2,128)(2,1)}), bf16[2,1024,2048]{2,0,1:T(2,128)(2,1)}, u32[]{:S(2)}, u32[]{:S(2)}) %all-to-all-start) | async-done | bytes 8388640 | tf_op jit(solution)/shard_map/all_to_all | solution.py:95
  136.5 11.2 %copy.56 = bf16[2,8,128,2048]{3,1,2,0:T(8,128)(2,1)} copy(bf16[2,8,128,2048]{3,0,2,1:T(2,128)(2,1)} %bitcast.1) | data formatting | bytes 16777216 | tf_op jit(solution)/shard_map/all_to_all | solution.py:95
  153.9 7.4 %squeeze.11 = bf16[128,128,128]{2,1,0:T(8,128)(2,1)} reshape(bf16[1,128,8,2048]{3,2,1,0:T(8,128)(2,1)} %get-tuple-element.24) | data formatting | bytes 8388608 | tf_op jit(solution)/shard_map/squeeze | solution.py:88
  161.3 7.1 %fusion.54 = f32[128,128,128]{2,0,1:T(8,128)} fusion(bf16[128,128,128]{2,1,0:T(8,128)(2,1)} %squeeze.11), kind=kOutput, calls=%fused_computation.88 | convolution fusion | flops 537133056 | bytes 12582912 | tf_op jit(solution)/shard_map/pa,rab->rpb/dot_general | solution.py:66
  173.0 7.4 %squeeze.10 = bf16[128,128,128]{2,1,0:T(8,128)(2,1)} reshape(bf16[1,128,8,2048]{3,2,1,0:T(8,128)(2,1)} %get-tuple-element.23) | data formatting | bytes 8388608 | tf_op jit(solution)/shard_map/squeeze | solution.py:88
  180.4 7.1 %fusion.52 = f32[128,128,128]{2,0,1:T(8,128)} fusion(bf16[128,128,128]{2,1,0:T(8,128)(2,1)} %squeeze.10), kind=kOutput, calls=%fused_computation.87 | convolution fusion | flops 537133056 | bytes 12582912 | tf_op jit(solution)/shard_map/pa,rab->rpb/dot_general | solution.py:69
  187.5 10.6 %fusion = (bf16[128,128,128]{2,1,0:T(8,128)(2,1)S(1)}, bf16[128,128,128]{2,1,0:T(8,128)(2,1)S(1)}) fusion(f32[128,128]{1,0:T(8,128)S(1)} %get-tuple-element.34, f32[128,128]{1,0:T(8,128)S(1)} %get-tuple-element.35, f32[128,128,128]{2,0,1:T(8,128)} %fusion.64, f32[128,128,128]{2,0,1:T(8,128)} %fusion.52, f32[128,128,128]{2,0,1:T(8,128)} %fusion.54, ...), kind=kOutput, calls=%fused_computation.30 | convolution fusion | flops 558104576 | bytes 37879808 | tf_op jit(solution)/shard_map/pa,rab->rpb/dot_general | solution.py:64
  220.4 6.6 %copy.31 = bf16[128,2,64,128]{3,2,1,0:T(8,128)(2,1)} copy(bf16[128,2,64,128]{0,3,2,1:T(8,128)(2,1)} %get-tuple-element.21) | data formatting | bytes 8388608 | tf_op jit(solution)/shard_map/split | solution.py:33
  226.9 20.6 %all-to-all-start.1 = ((bf16[128,2,64,128]{3,2,1,0:T(8,128)(2,1)}), bf16[128,2,64,128]{3,2,1,0:T(8,128)(2,1)}, u32[]{:S(2)}, u32[]{:S(2)}) async-start(bf16[128,2,64,128]{3,2,1,0:T(8,128)(2,1)} %copy.31), calls=%async_computation.1 | async-start | bytes 8388608 | tf_op jit(solution)/shard_map/all_to_all | solution.py:35
  254.0 42.8 %all-to-all-done.1 = bf16[128,2,64,128]{3,2,1,0:T(8,128)(2,1)} async-done(((bf16[128,2,64,128]{3,2,1,0:T(8,128)(2,1)}), bf16[128,2,64,128]{3,2,1,0:T(8,128)(2,1)}, u32[]{:S(2)}, u32[]{:S(2)}) %all-to-all-start.1) | async-done | bytes 4194336 | tf_op jit(solution)/shard_map/all_to_all | solution.py:35
  296.8 9.8 %all-to-all-start.2 = ((bf16[128,2,64,128]{3,2,1,0:T(8,128)(2,1)}), bf16[128,2,64,128]{3,2,1,0:T(8,128)(2,1)}, u32[]{:S(2)}, u32[]{:S(2)}) async-start(bf16[128,2,64,128]{3,2,1,0:T(8,128)(2,1)} %copy.32), calls=%async_computation.2 | async-start | bytes 8388608 | tf_op jit(solution)/shard_map/all_to_all | solution.py:35
  315.3 6.9 %copy.33 = bf16[128,2,64,128]{3,0,2,1:T(8,128)(2,1)} copy(bf16[128,2,64,128]{3,2,1,0:T(8,128)(2,1)} %all-to-all-done.1) | data formatting | bytes 8388608 | tf_op jit(solution)/shard_map/all_to_all | solution.py:35
  322.2 33.5 %all-to-all-done.2 = bf16[128,2,64,128]{3,2,1,0:T(8,128)(2,1)} async-done(((bf16[128,2,64,128]{3,2,1,0:T(8,128)(2,1)}), bf16[128,2,64,128]{3,2,1,0:T(8,128)(2,1)}, u32[]{:S(2)}, u32[]{:S(2)}) %all-to-all-start.2) | async-done | bytes 4194336 | tf_op jit(solution)/shard_map/all_to_all | solution.py:35
  355.7 6.9 %copy.34 = bf16[128,2,64,128]{3,0,2,1:T(8,128)(2,1)} copy(bf16[128,2,64,128]{3,2,1,0:T(8,128)(2,1)} %all-to-all-done.2) | data formatting | bytes 8388608 | tf_op jit(solution)/shard_map/all_to_all | solution.py:35
  362.6 7.5 %maximum_bitcast_fusion.1 = bf16[2,128,128,128]{3,1,2,0:T(8,128)(2,1)} fusion(bf16[128,2,64,128]{3,0,2,1:T(8,128)(2,1)} %copy.34, bf16[128,2,64,128]{3,0,2,1:T(8,128)(2,1)} %copy.33), kind=kLoop, calls=%fused_computation.19 | loop fusion | flops 4194304 | bytes 16777216 | tf_op jit(solution)/shard_map/transpose | solution.py:26
  384.1 9.0 %subtract_convert_fusion.1 = (bf16[128,128,128]{2,0,1:T(8,128)(2,1)S(1)}, bf16[128,128,128]{2,0,1:T(8,128)(2,1)S(1)}) fusion(f32[128,128]{0,1:T(8,128)S(1)} %copy.36, f32[128,128]{0,1:T(8,128)S(1)} %copy.35, f32[128,128,128]{2,0,1:T(8,128)S(1)} %fusion.5, f32[128,128,128]{2,0,1:T(8,128)} %fusion.6, f32[128,128,128]{2,0,1:T(8,128)} %fusion.8, ...), kind=kOutput, calls=%fused_computation.25 | convolution fusion | flops 558104576 | bytes 37879808 | tf_op jit(solution)/shard_map/pg,gic->pic/dot_general | solution.py:67
  393.1 6.7 %fusion.9 = f32[128,128,128]{2,0,1:T(8,128)} fusion(bf16[128,128,128]{2,0,1:T(8,128)(2,1)S(1)} %get-tuple-element.9), kind=kOutput, calls=%fused_computation.42 | convolution fusion | flops 537133056 | bytes 12582912 | tf_op jit(solution)/shard_map/qi,pic->qpc/dot_general | solution.py:67
  403.2 7.2 %add_convert_fusion = bf16[128,128,128]{2,0,1:T(8,128)(2,1)S(1)} fusion(f32[128,128,128]{2,0,1:T(8,128)} %fusion.9, bf16[128,128,128]{2,0,1:T(8,128)(2,1)S(1)} %get-tuple-element.8), kind=kOutput, calls=%fused_computation.22 | convolution fusion | flops 541327360 | bytes 16777216 | tf_op jit(solution)/shard_map/qi,pic->qpc/dot_general | solution.py:69
  435.3 10.5 %collective-permute-done = bf16[2,1024,128]{2,1,0:T(8,128)(2,1)} collective-permute-done((bf16[2,1024,128]{2,1,0:T(8,128)(2,1)S(1)}, bf16[2,1024,128]{2,1,0:T(8,128)(2,1)}, u32[]{:S(2)}, u32[]{:S(2)}) %collective-permute-start) | collective-permute-done | bytes 524320 | tf_op jit(solution)/shard_map/ppermute | solution.py:42
  461.0 18.3 %collective-permute-start.5 = (bf16[2,1024,128]{2,1,0:T(8,128)(2,1)}, bf16[2,1024,128]{2,1,0:T(8,128)(2,1)S(1)}, u32[]{:S(2)}, u32[]{:S(2)}) collective-permute-start(bf16[2,1024,128]{2,1,0:T(8,128)(2,1)} %get-tuple-element.20), channel_id=1, source_target_pairs={{2,0},{3,1},{4,2},{5,3},{6,4},{7,5},{8,6},{9,7},{10,8},{11,9},{12,... | collective-permute-start | bytes 1572872 | tf_op jit(solution)/shard_map/ppermute | solution.py:42
  493.7 11.5 %collective-permute-done.6 = bf16[2,1024,128]{2,1,0:T(8,128)(2,1)S(1)} collective-permute-done((bf16[2,1024,128]{2,1,0:T(8,128)(2,1)S(1)}, bf16[2,1024,128]{2,1,0:T(8,128)(2,1)S(1)}, u32[]{:S(2)}, u32[]{:S(2)}) %collective-permute-start.6) | collective-permute-done | bytes 524320 | tf_op jit(solution)/shard_map/ppermute | solution.py:42
  506.1 10.3 %collective-permute-done.7 = bf16[2,1024,128]{2,1,0:T(8,128)(2,1)S(1)} collective-permute-done((bf16[2,1024,128]{2,1,0:T(8,128)(2,1)S(1)}, bf16[2,1024,128]{2,1,0:T(8,128)(2,1)S(1)}, u32[]{:S(2)}, u32[]{:S(2)}) %collective-permute-start.7) | collective-permute-done | bytes 524320 | tf_op jit(solution)/shard_map/ppermute | solution.py:42
  517.3 6.9 %fusion.4 = bf16[1,2,1024,1024]{3,2,1,0:T(8,128)(2,1)} fusion(f32[1024,1024]{1,0:T(8,128)S(1)} %copy-done.6, bf16[2,1024,1152]{2,1,0:T(8,128)(2,1)} %constant_dynamic-update-slice_fusion, s32[]{:T(128)S(6)} %select_n.211), kind=kLoop, calls=%fused_computation.34 | loop fusion | flops 6291456 | bytes 12582916 | tf_op jit(solution)/shard_map/broadcast_in_dim | solution.py:130
  (73 shorter events, 113.3 us)
Async XLA Ops:
  16.4 120.1 %all-to-all-start = ((bf16[2,1024,2048]{2,0,1:T(2,128)(2,1)}), bf16[2,1024,2048]{2,0,1:T(2,128)(2,1)}, u32[]{:S(2)}, u32[]{:S(2)}) async-start(bf16[2,1024,2048]{2,0,1:T(2,128)(2,1)} %copy.29), calls=%async_computation | async-start | bytes 16777216 | tf_op jit(solution)/shard_map/all_to_all | solution.py:95
  161.3 7.1 %copy-start.2 = (bf16[128,128,128]{2,1,0:T(8,128)(2,1)S(1)}, bf16[128,128,128]{2,1,0:T(8,128)(2,1)}, u32[]{:S(2)}) copy-start(bf16[128,128,128]{2,1,0:T(8,128)(2,1)} %squeeze.11) | copy-start | bytes 12582916
  180.4 7.1 %copy-start.1 = (bf16[128,128,128]{2,1,0:T(8,128)(2,1)S(1)}, bf16[128,128,128]{2,1,0:T(8,128)(2,1)}, u32[]{:S(2)}) copy-start(bf16[128,128,128]{2,1,0:T(8,128)(2,1)} %squeeze.10) | copy-start | bytes 12582916
  204.5 3.5 copy-start.7
  226.9 69.8 %all-to-all-start.1 = ((bf16[128,2,64,128]{3,2,1,0:T(8,128)(2,1)}), bf16[128,2,64,128]{3,2,1,0:T(8,128)(2,1)}, u32[]{:S(2)}, u32[]{:S(2)}) async-start(bf16[128,2,64,128]{3,2,1,0:T(8,128)(2,1)} %copy.31), calls=%async_computation.1 | async-start | bytes 8388608 | tf_op jit(solution)/shard_map/all_to_all | solution.py:35
  254.0 53.0 %copy-start.9 = (s32[128]{0:T(128)S(1)}, s32[128]{0:T(128)}, u32[]{:S(2)}) copy-start(s32[128]{0:T(128)} %param.6) | copy-start | bytes 1540
  254.0 53.0 %copy-start.10 = (s32[128]{0:T(128)S(1)}, s32[128]{0:T(128)}, u32[]{:S(2)}) copy-start(s32[128]{0:T(128)} %param.7) | copy-start | bytes 1540
  254.0 53.0 %copy-start.11 = (s32[128]{0:T(128)S(1)}, s32[128]{0:T(128)}, u32[]{:S(2)}) copy-start(s32[128]{0:T(128)} %param.5) | copy-start | bytes 1540
  296.8 58.9 %all-to-all-start.2 = ((bf16[128,2,64,128]{3,2,1,0:T(8,128)(2,1)}), bf16[128,2,64,128]{3,2,1,0:T(8,128)(2,1)}, u32[]{:S(2)}, u32[]{:S(2)}) async-start(bf16[128,2,64,128]{3,2,1,0:T(8,128)(2,1)} %copy.32), calls=%async_computation.2 | async-start | bytes 8388608 | tf_op jit(solution)/shard_map/all_to_all | solution.py:35
  370.0 4.6 copy-start
  413.4 6.5 %copy-start.3 = (bf16[128,128,128]{2,1,0:T(8,128)(2,1)}, bf16[128,128,128]{2,1,0:T(8,128)(2,1)S(1)}, u32[]{:S(2)}) copy-start(bf16[128,128,128]{2,1,0:T(8,128)(2,1)S(1)} %copy.42) | copy-start | bytes 12582916
  419.9 2.0 copy-start.5
  421.9 23.8 %collective-permute-start = (bf16[2,1024,128]{2,1,0:T(8,128)(2,1)S(1)}, bf16[2,1024,128]{2,1,0:T(8,128)(2,1)}, u32[]{:S(2)}, u32[]{:S(2)}) collective-permute-start(bf16[2,1024,128]{2,1,0:T(8,128)(2,1)S(1)} %get-tuple-element.13), channel_id=1, source_target_pairs={{124,0},{125,1},{126,2},{127,3},{0,4},{1,5},{2,6},{3,7},{4,8},{5,9... | collective-permute-start | bytes 1572872 | tf_op jit(solution)/shard_map/ppermute | solution.py:42
  423.3 23.6 %collective-permute-start.1 = (bf16[2,1024,128]{2,1,0:T(8,128)(2,1)S(1)}, bf16[2,1024,128]{2,1,0:T(8,128)(2,1)}, u32[]{:S(2)}, u32[]{:S(2)}) collective-permute-start(bf16[2,1024,128]{2,1,0:T(8,128)(2,1)S(1)} %get-tuple-element.14), channel_id=1, source_target_pairs={{125,0},{126,1},{127,2},{0,3},{1,4},{2,5},{3,6},{4,7},{5,8},{6,9},... | collective-permute-start | bytes 1572872 | tf_op jit(solution)/shard_map/ppermute | solution.py:42
  426.7 21.4 %collective-permute-start.2 = (bf16[2,1024,128]{2,1,0:T(8,128)(2,1)S(1)}, bf16[2,1024,128]{2,1,0:T(8,128)(2,1)}, u32[]{:S(2)}, u32[]{:S(2)}) collective-permute-start(bf16[2,1024,128]{2,1,0:T(8,128)(2,1)S(1)} %get-tuple-element.15), channel_id=1, source_target_pairs={{126,0},{127,1},{0,2},{1,3},{2,4},{3,5},{4,6},{5,7},{6,8},{7,9},{8... | collective-permute-start | bytes 1572872 | tf_op jit(solution)/shard_map/ppermute | solution.py:42
  428.6 26.7 %collective-permute-start.3 = (bf16[2,1024,128]{2,1,0:T(8,128)(2,1)S(1)}, bf16[2,1024,128]{2,1,0:T(8,128)(2,1)}, u32[]{:S(2)}, u32[]{:S(2)}) collective-permute-start(bf16[2,1024,128]{2,1,0:T(8,128)(2,1)S(1)} %get-tuple-element.16), channel_id=1, source_target_pairs={{127,0},{0,1},{1,2},{2,3},{3,4},{4,5},{5,6},{6,7},{7,8},{8,9},{9,1... | collective-permute-start | bytes 1572872 | tf_op jit(solution)/shard_map/ppermute | solution.py:42
  434.5 22.0 %copy-start.4 = (bf16[128,128,128]{2,1,0:T(8,128)(2,1)S(1)}, bf16[128,128,128]{2,1,0:T(8,128)(2,1)}, u32[]{:S(2)}) copy-start(bf16[128,128,128]{2,1,0:T(8,128)(2,1)} %copy-done.3) | copy-start | bytes 12582916
  434.5 53.6 %collective-permute-start.4 = (bf16[2,1024,128]{2,1,0:T(8,128)(2,1)S(1)}, bf16[2,1024,128]{2,1,0:T(8,128)(2,1)}, u32[]{:S(2)}, u32[]{:S(2)}) collective-permute-start(bf16[2,1024,128]{2,1,0:T(8,128)(2,1)S(1)} %get-tuple-element.17), channel_id=1, source_target_pairs={{1,0},{2,1},{3,2},{4,3},{5,4},{6,5},{7,6},{8,7},{9,8},{10,9},{11,1... | collective-permute-start | bytes 1572872 | tf_op jit(solution)/shard_map/ppermute | solution.py:42
  458.9 2.1 copy-start.8
  461.0 31.8 %collective-permute-start.5 = (bf16[2,1024,128]{2,1,0:T(8,128)(2,1)}, bf16[2,1024,128]{2,1,0:T(8,128)(2,1)S(1)}, u32[]{:S(2)}, u32[]{:S(2)}) collective-permute-start(bf16[2,1024,128]{2,1,0:T(8,128)(2,1)} %get-tuple-element.20), channel_id=1, source_target_pairs={{2,0},{3,1},{4,2},{5,3},{6,4},{7,5},{8,6},{9,7},{10,8},{11,9},{12,... | collective-permute-start | bytes 1572872 | tf_op jit(solution)/shard_map/ppermute | solution.py:42
  479.4 37.0 %collective-permute-start.7 = (bf16[2,1024,128]{2,1,0:T(8,128)(2,1)S(1)}, bf16[2,1024,128]{2,1,0:T(8,128)(2,1)S(1)}, u32[]{:S(2)}, u32[]{:S(2)}) collective-permute-start(bf16[2,1024,128]{2,1,0:T(8,128)(2,1)S(1)} %get-tuple-element.12), channel_id=1, source_target_pairs={{4,0},{5,1},{6,2},{7,3},{8,4},{9,5},{10,6},{11,7},{12,8},{13,9},{1... | collective-permute-start | bytes 1572872 | tf_op jit(solution)/shard_map/ppermute | solution.py:42
  483.1 22.1 %collective-permute-start.6 = (bf16[2,1024,128]{2,1,0:T(8,128)(2,1)S(1)}, bf16[2,1024,128]{2,1,0:T(8,128)(2,1)S(1)}, u32[]{:S(2)}, u32[]{:S(2)}) collective-permute-start(bf16[2,1024,128]{2,1,0:T(8,128)(2,1)S(1)} %get-tuple-element.18), channel_id=1, source_target_pairs={{3,0},{4,1},{5,2},{6,3},{7,4},{8,5},{9,6},{10,7},{11,8},{12,9},{13... | collective-permute-start | bytes 1572872 | tf_op jit(solution)/shard_map/ppermute | solution.py:42
  488.1 29.2 %copy-start.6 = (f32[1024,1024]{1,0:T(8,128)S(1)}, f32[1024,1024]{1,0:T(8,128)}, u32[]{:S(2)}) copy-start(f32[1024,1024]{1,0:T(8,128)} %multiply_multiply_fusion) | copy-start | bytes 12582916
where the time goes:
time: 534 us; the launch traced here: 525 us
  waiting for transfers between devices  232 us (43%)
  local copies, waits for them, and re-layouts  103 us (19%)
  matrix products  82.6 us (15%)
  starting transfers between devices  66 us (12%)
  other arithmetic  27 us (5%)
  between operations  14.5 us (3%)
    all_to_all x1, waiting for transfers between devices, shards(): lax.all_to_all(sky_image, 'col', split_axis=1, concat_axis=2, tiled=True)  115 us
    all_to_all x2, waiting for transfers between devices, cut_exchange(): lax.all_to_all(share, axis, split_axis=0, concat_axis=0, tiled=True)  76.2 us
    ppermute x8, waiting for transfers between devices, shifted(): return lax.ppermute(block, axis, route)  41 us
    ppermute x8, starting transfers between devices, shifted(): return lax.ppermute(block, axis, route)  30.5 us
    all_to_all x2, starting transfers between devices, cut_exchange(): lax.all_to_all(share, axis, split_axis=0, concat_axis=0, tiled=True)  30.4 us
    unnamed x32, local copies, waits for them, and re-layouts  28.9 us
    dot_general x4, matrix products, complex_mix(): jnp.einsum(formula, tables[0], values[1], preferred_element_type=jnp.floa...  21.9 us
    dot_general x4, matrix products, complex_mix(): jnp.einsum(formula, tables[1], values[0], preferred_element_type=jnp.floa...  21.6 us
  transfers between devices with their start and end apart: 11, of which 8 were waited for; matrix products, arithmetic and copies ran while one was open for 6% of the time, Pallas kernels for 0%

commit v1 on v0

--- a/solution.py
+++ b/solution.py
@@ -92,7 +92,10 @@
 
 
 def shards(sky_image, facet_rows, facet_offsets, facet_owner):
-    strip_rows = lax.all_to_all(sky_image, "col", split_axis=1, concat_axis=2, tiled=True)
+    strip_rows = jnp.concatenate(
+        lax.all_to_all(jnp.stack(jnp.split(sky_image, lax.axis_size("col"), axis=1)), "col", 0, 0),
+        axis=2,
+    )
     rows_done = rows_pass(strip_rows)
     row_devices = lax.axis_size("row")
     col_devices = lax.axis_size("col")

time: 534 us -> 550 us (1.030)
  local copies, waits for them, and re-layouts: 103 us -> 114 us
    unnamed x32 -> x52, local copies, waits for them, and re-layouts: 28.9 us -> 38.3 us
    dot_general x4, matrix products: 21.9 us -> 29.9 us  [complex_mix(): jnp.einsum(formula, tables[0], values[1], preferred_element_type=jnp.floa...]
    dot_general x4, matrix products: 20.6 us -> 14.7 us  [complex_mix(): jnp.einsum(formula, tables[0], values[0], preferred_element_type=jnp.floa...]
    split x0 -> x1, local copies, waits for them, and re-layouts: none -> 5.6 us  [shards(): jnp.split(sky_image, lax.axis_size('col'), axis=1)]
  transfers between devices with their start and end apart: 11 -> 11, of which waited for: 8 -> 8; matrix products, arithmetic and copies ran while one was open for 6% -> 5% of each run, Pallas kernels for 0% -> 0%
where the time goes in v1:
time: 550 us; the launch traced here: 540 us
  waiting for transfers between devices  232 us (42%)
  local copies, waits for them, and re-layouts  114 us (21%)
  matrix products  85.1 us (15%)
  starting transfers between devices  65.9 us (12%)
  other arithmetic  28.6 us (5%)
  between operations  14.1 us (3%)
    all_to_all x1, waiting for transfers between devices, shards(): lax.all_to_all(jnp.stack(jnp.split(sky_image, lax.axis_size('col'), axis=...  114 us
    all_to_all x2, waiting for transfers between devices, cut_exchange(): lax.all_to_all(share, axis, split_axis=0, concat_axis=0, tiled=True)  76.8 us
    ppermute x8, waiting for transfers between devices, shifted(): return lax.ppermute(block, axis, route)  41.2 us
    unnamed x52, local copies, waits for them, and re-layouts  38.3 us
    ppermute x8, starting transfers between devices, shifted(): return lax.ppermute(block, axis, route)  30.4 us
    all_to_all x2, starting transfers between devices, cut_exchange(): lax.all_to_all(share, axis, split_axis=0, concat_axis=0, tiled=True)  30.4 us
    dot_general x4, matrix products, complex_mix(): jnp.einsum(formula, tables[0], values[1], preferred_element_type=jnp.floa...  29.9 us
    dot_general x4, matrix products, complex_mix(): jnp.einsum(formula, tables[1], values[0], preferred_element_type=jnp.floa...  22.7 us
  transfers between devices with their start and end apart: 11, of which 8 were waited for; matrix products, arithmetic and copies ran while one was open for 5% of the time, Pallas kernels for 0%

profile of v1, /device:TPU:21, one launch (start us, length us, event | category | flops | bytes accessed | tf_op | source)
XLA Modules:
  0.0 540.4 jit_solution(2547450172804181989)
XLA Ops:
  37.8 114.4 %all-to-all-done = bf16[8,2,128,2048]{2,3,1,0:T(8,128)(2,1)} async-done(((bf16[8,2,128,2048]{2,3,1,0:T(8,128)(2,1)}), bf16[8,2,128,2048]{2,3,1,0:T(8,128)(2,1)}, u32[]{:S(2)}, u32[]{:S(2)}) %all-to-all-start) | async-done | bytes 8388640 | tf_op jit(solution)/shard_map/all_to_all | solution.py:96
  152.2 7.5 %copy.107 = bf16[8,2,128,2048]{2,3,0,1:T(8,128)(2,1)} copy(bf16[8,2,128,2048]{2,3,1,0:T(8,128)(2,1)} %all-to-all-done) | data formatting | bytes 16777216 | tf_op jit(solution)/shard_map/all_to_all | solution.py:96
  165.5 7.3 %copy.60 = bf16[128,128,128]{1,2,0:T(8,128)(2,1)} copy(bf16[128,128,128]{0,2,1:T(8,128)(2,1)} %bitcast.123) | data formatting | bytes 8388608 | tf_op jit(solution)/shard_map/squeeze | solution.py:88
  172.8 7.1 %fusion.54 = f32[128,128,128]{2,1,0:T(8,128)} fusion(bf16[128,128,128]{1,2,0:T(8,128)(2,1)} %copy.60), kind=kOutput, calls=%fused_computation.107 | convolution fusion | flops 537133056 | bytes 12582912 | tf_op jit(solution)/shard_map/pa,rab->rpb/dot_general | solution.py:69
  184.6 7.2 %copy.61 = bf16[128,128,128]{1,2,0:T(8,128)(2,1)} copy(bf16[128,128,128]{0,2,1:T(8,128)(2,1)} %bitcast.122) | data formatting | bytes 8388608 | tf_op jit(solution)/shard_map/squeeze | solution.py:88
  191.8 7.1 %fusion.56 = f32[128,128,128]{2,1,0:T(8,128)} fusion(bf16[128,128,128]{1,2,0:T(8,128)(2,1)} %copy.61), kind=kOutput, calls=%fused_computation.108 | convolution fusion | flops 537133056 | bytes 12582912 | tf_op jit(solution)/shard_map/pa,rab->rpb/dot_general | solution.py:66
  198.9 12.6 %fusion.1 = (bf16[128,128,128]{1,2,0:T(8,128)(2,1)S(1)}, bf16[128,128,128]{1,2,0:T(8,128)(2,1)}) fusion(f32[128,128]{0,1:T(8,128)S(1)} %copy.65, f32[128,128]{0,1:T(8,128)S(1)} %copy.62, f32[128,128,128]{2,1,0:T(8,128)} %fusion.54, f32[128,128,128]{2,1,0:T(8,128)} %fusion.68, f32[128,128,128]{2,1,0:T(8,128)} %fusion.56, bf16[128,128,128]{1,2,0:T(8,128)(2,1)S(1)} %copy-done.1), kind=kOutput, calls=%fused_computation.23 | convolution fusion | flops 558104576 | bytes 37879808 | tf_op jit(solution)/shard_map/pa,rab->rpb/dot_general | solution.py:67
  222.3 7.5 %maximum_bitcast_fusion = bf16[128,2,128,128]{0,3,2,1:T(8,128)(2,1)} fusion(bf16[1,128,128,128]{2,3,1,0:T(8,128)(2,1)} %fusion.5, bf16[1,128,128,128]{2,3,1,0:T(8,128)(2,1)} %fusion.4), kind=kLoop, calls=%fused_computation.18 | loop fusion | flops 4194304 | bytes 16777216 | tf_op jit(solution)/shard_map/transpose | solution.py:15
  236.0 6.6 %copy.70 = bf16[128,2,64,128]{3,2,1,0:T(8,128)(2,1)} copy(bf16[128,2,64,128]{0,3,2,1:T(8,128)(2,1)} %get-tuple-element.21) | data formatting | bytes 8388608 | tf_op jit(solution)/shard_map/split | solution.py:33
  242.6 20.5 %all-to-all-start.1 = ((bf16[128,2,64,128]{3,2,1,0:T(8,128)(2,1)}), bf16[128,2,64,128]{3,2,1,0:T(8,128)(2,1)}, u32[]{:S(2)}, u32[]{:S(2)}) async-start(bf16[128,2,64,128]{3,2,1,0:T(8,128)(2,1)} %copy.70), calls=%async_computation.1 | async-start | bytes 8388608 | tf_op jit(solution)/shard_map/all_to_all | solution.py:35
  269.6 42.8 %all-to-all-done.1 = bf16[128,2,64,128]{3,2,1,0:T(8,128)(2,1)} async-done(((bf16[128,2,64,128]{3,2,1,0:T(8,128)(2,1)}), bf16[128,2,64,128]{3,2,1,0:T(8,128)(2,1)}, u32[]{:S(2)}, u32[]{:S(2)}) %all-to-all-start.1) | async-done | bytes 4194336 | tf_op jit(solution)/shard_map/all_to_all | solution.py:35
  312.4 9.8 %all-to-all-start.2 = ((bf16[128,2,64,128]{3,2,1,0:T(8,128)(2,1)}), bf16[128,2,64,128]{3,2,1,0:T(8,128)(2,1)}, u32[]{:S(2)}, u32[]{:S(2)}) async-start(bf16[128,2,64,128]{3,2,1,0:T(8,128)(2,1)} %copy.71), calls=%async_computation.2 | async-start | bytes 8388608 | tf_op jit(solution)/shard_map/all_to_all | solution.py:35
  330.4 6.9 %copy.72 = bf16[128,2,64,128]{3,0,2,1:T(8,128)(2,1)} copy(bf16[128,2,64,128]{3,2,1,0:T(8,128)(2,1)} %all-to-all-done.1) | data formatting | bytes 8388608 | tf_op jit(solution)/shard_map/all_to_all | solution.py:35
  337.3 34.0 %all-to-all-done.2 = bf16[128,2,64,128]{3,2,1,0:T(8,128)(2,1)} async-done(((bf16[128,2,64,128]{3,2,1,0:T(8,128)(2,1)}), bf16[128,2,64,128]{3,2,1,0:T(8,128)(2,1)}, u32[]{:S(2)}, u32[]{:S(2)}) %all-to-all-start.2) | async-done | bytes 4194336 | tf_op jit(solution)/shard_map/all_to_all | solution.py:35
  371.3 6.9 %copy.73 = bf16[128,2,64,128]{3,0,2,1:T(8,128)(2,1)} copy(bf16[128,2,64,128]{3,2,1,0:T(8,128)(2,1)} %all-to-all-done.2) | data formatting | bytes 8388608 | tf_op jit(solution)/shard_map/all_to_all | solution.py:35
  378.2 7.5 %maximum_bitcast_fusion.1 = bf16[2,128,128,128]{3,1,2,0:T(8,128)(2,1)} fusion(bf16[128,2,64,128]{3,0,2,1:T(8,128)(2,1)} %copy.73, bf16[128,2,64,128]{3,0,2,1:T(8,128)(2,1)} %copy.72), kind=kLoop, calls=%fused_computation.19 | loop fusion | flops 4194304 | bytes 16777216 | tf_op jit(solution)/shard_map/transpose | solution.py:26
  399.7 9.1 %subtract_convert_fusion.1 = (bf16[128,128,128]{2,0,1:T(8,128)(2,1)S(1)}, bf16[128,128,128]{2,0,1:T(8,128)(2,1)S(1)}) fusion(f32[128,128]{0,1:T(8,128)S(1)} %copy.65, f32[128,128]{0,1:T(8,128)S(1)} %copy.62, f32[128,128,128]{2,0,1:T(8,128)} %fusion.7, f32[128,128,128]{2,0,1:T(8,128)} %fusion.8, f32[128,128,128]{2,0,1:T(8,128)S(1)} %fusion.10, ...), kind=kOutput, calls=%fused_computation.33 | convolution fusion | flops 558104576 | bytes 37879808 | tf_op jit(solution)/shard_map/pg,gic->pic/dot_general | solution.py:67
  408.8 6.7 %fusion.11 = f32[128,128,128]{2,0,1:T(8,128)} fusion(bf16[128,128,128]{2,0,1:T(8,128)(2,1)S(1)} %get-tuple-element.9), kind=kOutput, calls=%fused_computation.46 | convolution fusion | flops 537133056 | bytes 12582912 | tf_op jit(solution)/shard_map/qi,pic->qpc/dot_general | solution.py:67
  418.9 7.2 %add_convert_fusion = bf16[128,128,128]{2,0,1:T(8,128)(2,1)S(1)} fusion(f32[128,128,128]{2,0,1:T(8,128)} %fusion.11, bf16[128,128,128]{2,0,1:T(8,128)(2,1)S(1)} %get-tuple-element.8), kind=kOutput, calls=%fused_computation.30 | convolution fusion | flops 541327360 | bytes 16777216 | tf_op jit(solution)/shard_map/qi,pic->qpc/dot_general | solution.py:69
  450.7 10.8 %collective-permute-done = bf16[2,1024,128]{2,1,0:T(8,128)(2,1)} collective-permute-done((bf16[2,1024,128]{2,1,0:T(8,128)(2,1)S(1)}, bf16[2,1024,128]{2,1,0:T(8,128)(2,1)}, u32[]{:S(2)}, u32[]{:S(2)}) %collective-permute-start) | collective-permute-done | bytes 524320 | tf_op jit(solution)/shard_map/ppermute | solution.py:42
  476.8 18.2 %collective-permute-start.5 = (bf16[2,1024,128]{2,1,0:T(8,128)(2,1)}, bf16[2,1024,128]{2,1,0:T(8,128)(2,1)S(1)}, u32[]{:S(2)}, u32[]{:S(2)}) collective-permute-start(bf16[2,1024,128]{2,1,0:T(8,128)(2,1)} %get-tuple-element.20), channel_id=1, source_target_pairs={{2,0},{3,1},{4,2},{5,3},{6,4},{7,5},{8,6},{9,7},{10,8},{11,9},{12,... | collective-permute-start | bytes 1572872 | tf_op jit(solution)/shard_map/ppermute | solution.py:42
  509.4 11.5 %collective-permute-done.6 = bf16[2,1024,128]{2,1,0:T(8,128)(2,1)S(1)} collective-permute-done((bf16[2,1024,128]{2,1,0:T(8,128)(2,1)S(1)}, bf16[2,1024,128]{2,1,0:T(8,128)(2,1)S(1)}, u32[]{:S(2)}, u32[]{:S(2)}) %collective-permute-start.6) | collective-permute-done | bytes 524320 | tf_op jit(solution)/shard_map/ppermute | solution.py:42
  521.9 10.2 %collective-permute-done.7 = bf16[2,1024,128]{2,1,0:T(8,128)(2,1)S(1)} collective-permute-done((bf16[2,1024,128]{2,1,0:T(8,128)(2,1)S(1)}, bf16[2,1024,128]{2,1,0:T(8,128)(2,1)S(1)}, u32[]{:S(2)}, u32[]{:S(2)}) %collective-permute-start.7) | collective-permute-done | bytes 524320 | tf_op jit(solution)/shard_map/ppermute | solution.py:42
  533.0 6.9 %fusion.6 = bf16[1,2,1024,1024]{3,2,1,0:T(8,128)(2,1)} fusion(f32[1024,1024]{1,0:T(8,128)S(1)} %copy-done.7, bf16[2,1024,1152]{2,1,0:T(8,128)(2,1)} %constant_dynamic-update-slice_fusion, s32[]{:T(128)S(6)} %select_n.211), kind=kLoop, calls=%fused_computation.38 | loop fusion | flops 6291456 | bytes 12582916 | tf_op jit(solution)/shard_map/broadcast_in_dim | solution.py:133
  (96 shorter events, 139.9 us)
Async XLA Ops:
  21.9 4.7 copy-start.11
  21.9 5.7 %copy-start.10 = (bf16[2,128,2048]{1,2,0:T(8,128)(2,1)S(1)}, bf16[2,128,2048]{1,2,0:T(8,128)(2,1)}, u32[]{:S(2)}) copy-start(bf16[2,128,2048]{1,2,0:T(8,128)(2,1)} %copy.90) | copy-start | bytes 3145732
  21.9 6.8 %copy-start.9 = (bf16[2,128,2048]{1,2,0:T(8,128)(2,1)S(1)}, bf16[2,128,2048]{1,2,0:T(8,128)(2,1)}, u32[]{:S(2)}) copy-start(bf16[2,128,2048]{1,2,0:T(8,128)(2,1)} %copy.91) | copy-start | bytes 3145732
  32.0 120.2 %all-to-all-start = ((bf16[8,2,128,2048]{2,3,1,0:T(8,128)(2,1)}), bf16[8,2,128,2048]{2,3,1,0:T(8,128)(2,1)}, u32[]{:S(2)}, u32[]{:S(2)}) async-start(bf16[8,2,128,2048]{2,3,1,0:T(8,128)(2,1)} %bitcast_dynamic-update-slice_fusion), calls=%async_computation | async-start | bytes 16777216 | tf_op jit(solution)/shard_map/all_to_all | solution.py:96
  172.8 7.1 %copy-start.2 = (bf16[128,128,128]{1,2,0:T(8,128)(2,1)S(1)}, bf16[128,128,128]{1,2,0:T(8,128)(2,1)}, u32[]{:S(2)}) copy-start(bf16[128,128,128]{1,2,0:T(8,128)(2,1)} %copy.60) | copy-start | bytes 12582916
  191.8 7.1 %copy-start.1 = (bf16[128,128,128]{1,2,0:T(8,128)(2,1)S(1)}, bf16[128,128,128]{1,2,0:T(8,128)(2,1)}, u32[]{:S(2)}) copy-start(bf16[128,128,128]{1,2,0:T(8,128)(2,1)} %copy.61) | copy-start | bytes 12582916
  211.5 2.2 copy-start.6
  242.6 69.8 %all-to-all-start.1 = ((bf16[128,2,64,128]{3,2,1,0:T(8,128)(2,1)}), bf16[128,2,64,128]{3,2,1,0:T(8,128)(2,1)}, u32[]{:S(2)}, u32[]{:S(2)}) async-start(bf16[128,2,64,128]{3,2,1,0:T(8,128)(2,1)} %copy.70), calls=%async_computation.1 | async-start | bytes 8388608 | tf_op jit(solution)/shard_map/all_to_all | solution.py:35
  269.6 52.8 %copy-start.12 = (s32[128]{0:T(128)S(1)}, s32[128]{0:T(128)}, u32[]{:S(2)}) copy-start(s32[128]{0:T(128)} %param.6) | copy-start | bytes 1540
  269.6 52.8 %copy-start.13 = (s32[128]{0:T(128)S(1)}, s32[128]{0:T(128)}, u32[]{:S(2)}) copy-start(s32[128]{0:T(128)} %param.7) | copy-start | bytes 1540
  269.6 52.8 %copy-start.14 = (s32[128]{0:T(128)S(1)}, s32[128]{0:T(128)}, u32[]{:S(2)}) copy-start(s32[128]{0:T(128)} %param.5) | copy-start | bytes 1540
  312.4 58.9 %all-to-all-start.2 = ((bf16[128,2,64,128]{3,2,1,0:T(8,128)(2,1)}), bf16[128,2,64,128]{3,2,1,0:T(8,128)(2,1)}, u32[]{:S(2)}, u32[]{:S(2)}) async-start(bf16[128,2,64,128]{3,2,1,0:T(8,128)(2,1)} %copy.71), calls=%async_computation.2 | async-start | bytes 8388608 | tf_op jit(solution)/shard_map/all_to_all | solution.py:35
  385.6 4.6 copy-start
  429.1 6.5 %copy-start.3 = (bf16[128,128,128]{2,1,0:T(8,128)(2,1)}, bf16[128,128,128]{2,1,0:T(8,128)(2,1)S(1)}, u32[]{:S(2)}) copy-start(bf16[128,128,128]{2,1,0:T(8,128)(2,1)S(1)} %copy.81) | copy-start | bytes 12582916
  437.6 23.9 %collective-permute-start = (bf16[2,1024,128]{2,1,0:T(8,128)(2,1)S(1)}, bf16[2,1024,128]{2,1,0:T(8,128)(2,1)}, u32[]{:S(2)}, u32[]{:S(2)}) collective-permute-start(bf16[2,1024,128]{2,1,0:T(8,128)(2,1)S(1)} %get-tuple-element.13), channel_id=1, source_target_pairs={{124,0},{125,1},{126,2},{127,3},{0,4},{1,5},{2,6},{3,7},{4,8},{5,9... | collective-permute-start | bytes 1572872 | tf_op jit(solution)/shard_map/ppermute | solution.py:42
  439.0 23.6 %collective-permute-start.1 = (bf16[2,1024,128]{2,1,0:T(8,128)(2,1)S(1)}, bf16[2,1024,128]{2,1,0:T(8,128)(2,1)}, u32[]{:S(2)}, u32[]{:S(2)}) collective-permute-start(bf16[2,1024,128]{2,1,0:T(8,128)(2,1)S(1)} %get-tuple-element.14), channel_id=1, source_target_pairs={{125,0},{126,1},{127,2},{0,3},{1,4},{2,5},{3,6},{4,7},{5,8},{6,9},... | collective-permute-start | bytes 1572872 | tf_op jit(solution)/shard_map/ppermute | solution.py:42
  442.4 21.4 %collective-permute-start.2 = (bf16[2,1024,128]{2,1,0:T(8,128)(2,1)S(1)}, bf16[2,1024,128]{2,1,0:T(8,128)(2,1)}, u32[]{:S(2)}, u32[]{:S(2)}) collective-permute-start(bf16[2,1024,128]{2,1,0:T(8,128)(2,1)S(1)} %get-tuple-element.15), channel_id=1, source_target_pairs={{126,0},{127,1},{0,2},{1,3},{2,4},{3,5},{4,6},{5,7},{6,8},{7,9},{8... | collective-permute-start | bytes 1572872 | tf_op jit(solution)/shard_map/ppermute | solution.py:42
  444.3 26.7 %collective-permute-start.3 = (bf16[2,1024,128]{2,1,0:T(8,128)(2,1)S(1)}, bf16[2,1024,128]{2,1,0:T(8,128)(2,1)}, u32[]{:S(2)}, u32[]{:S(2)}) collective-permute-start(bf16[2,1024,128]{2,1,0:T(8,128)(2,1)S(1)} %get-tuple-element.16), channel_id=1, source_target_pairs={{127,0},{0,1},{1,2},{2,3},{3,4},{4,5},{5,6},{6,7},{7,8},{8,9},{9,1... | collective-permute-start | bytes 1572872 | tf_op jit(solution)/shard_map/ppermute | solution.py:42
  449.9 22.3 %copy-start.4 = (bf16[128,128,128]{2,1,0:T(8,128)(2,1)S(1)}, bf16[128,128,128]{2,1,0:T(8,128)(2,1)}, u32[]{:S(2)}) copy-start(bf16[128,128,128]{2,1,0:T(8,128)(2,1)} %copy-done.3) | copy-start | bytes 12582916
  449.9 54.0 %collective-permute-start.4 = (bf16[2,1024,128]{2,1,0:T(8,128)(2,1)S(1)}, bf16[2,1024,128]{2,1,0:T(8,128)(2,1)}, u32[]{:S(2)}, u32[]{:S(2)}) collective-permute-start(bf16[2,1024,128]{2,1,0:T(8,128)(2,1)S(1)} %get-tuple-element.17), channel_id=1, source_target_pairs={{1,0},{2,1},{3,2},{4,3},{5,4},{6,5},{7,6},{8,7},{9,8},{10,9},{11,1... | collective-permute-start | bytes 1572872 | tf_op jit(solution)/shard_map/ppermute | solution.py:42
  476.8 31.7 %collective-permute-start.5 = (bf16[2,1024,128]{2,1,0:T(8,128)(2,1)}, bf16[2,1024,128]{2,1,0:T(8,128)(2,1)S(1)}, u32[]{:S(2)}, u32[]{:S(2)}) collective-permute-start(bf16[2,1024,128]{2,1,0:T(8,128)(2,1)} %get-tuple-element.20), channel_id=1, source_target_pairs={{2,0},{3,1},{4,2},{5,3},{6,4},{7,5},{8,6},{9,7},{10,8},{11,9},{12,... | collective-permute-start | bytes 1572872 | tf_op jit(solution)/shard_map/ppermute | solution.py:42
  495.1 37.0 %collective-permute-start.7 = (bf16[2,1024,128]{2,1,0:T(8,128)(2,1)S(1)}, bf16[2,1024,128]{2,1,0:T(8,128)(2,1)S(1)}, u32[]{:S(2)}, u32[]{:S(2)}) collective-permute-start(bf16[2,1024,128]{2,1,0:T(8,128)(2,1)S(1)} %get-tuple-element.12), channel_id=1, source_target_pairs={{4,0},{5,1},{6,2},{7,3},{8,4},{9,5},{10,6},{11,7},{12,8},{13,9},{1... | collective-permute-start | bytes 1572872 | tf_op jit(solution)/shard_map/ppermute | solution.py:42
  498.8 22.1 %collective-permute-start.6 = (bf16[2,1024,128]{2,1,0:T(8,128)(2,1)S(1)}, bf16[2,1024,128]{2,1,0:T(8,128)(2,1)S(1)}, u32[]{:S(2)}, u32[]{:S(2)}) collective-permute-start(bf16[2,1024,128]{2,1,0:T(8,128)(2,1)S(1)} %get-tuple-element.18), channel_id=1, source_target_pairs={{3,0},{4,1},{5,2},{6,3},{7,4},{8,5},{9,6},{10,7},{11,8},{12,9},{13... | collective-permute-start | bytes 1572872 | tf_op jit(solution)/shard_map/ppermute | solution.py:42
  503.9 29.1 %copy-start.7 = (f32[1024,1024]{1,0:T(8,128)S(1)}, f32[1024,1024]{1,0:T(8,128)}, u32[]{:S(2)}) copy-start(f32[1024,1024]{1,0:T(8,128)} %multiply_multiply_fusion) | copy-start | bytes 12582916
  (2 other events, 4.2 us)
